TPU v7x, 32 devices: a whole 2x2x4 slice. The times are simulated.
32 devices in a mesh: inputs: 8 (over z, y), tm: 4 (over x, core).
Axes of the slice: x: 2, y: 2, z: 4, core: 2. Of those that a mesh axis runs over, the one named last changes fastest.
Arguments:
- voltages: bfloat16 [128, 131072], P('inputs', 'tm'), may hold values from -8 to 8
- pfb_taps: float32 [8, 512], replicated, may hold values from -2 to 2
Outputs:
- visibilities: float32 [256, 1, 2, 128, 128], P(('inputs', 'tm'))
All inputs are finite; a program needn't handle non-finite values.
Results may differ from a plain program's by a relative error of at most 0.002.
Values may be sent and summed in bfloat16 or wider, within the bound.
No kernel may reach another device: no remote copies, remote signals or barrier semaphores. Data moves between devices by JAX's collectives and lax.ppermute only.
A program may use at most 128 MiB of HBM per device.

v0:
```python
import jax
import jax.numpy as jnp
from jax import lax
from jax.sharding import PartitionSpec as P

F = 256
TAPS = 8
TILE = 128
FRAME = 512


def from_behind(value, axis, steps):
    count = lax.axis_size(axis)
    initial, last = (max(0, -steps), min(count, count - steps))
    return lax.ppermute(value, axis, [(source, source + steps) for source in range(initial, last)])


def dft_table(chans, length):
    rows = jnp.arange(2 * chans, dtype=jnp.int32)
    freq = rows // 2
    part = rows % 2
    samp = jnp.arange(length, dtype=jnp.int32)
    phase = freq[:, None] * samp[None, :] % length
    angle = 2.0 * jnp.pi / length * phase.astype(jnp.float32)
    vals = jnp.where(part[:, None] == 0, jnp.cos(angle), -jnp.sin(angle))
    return (vals * (1.0 / length**0.5)).astype(jnp.bfloat16)


def tile_sums(spec, scale):
    left = jnp.concatenate([spec[:, 0], spec[:, 1]], axis=-1)
    twisted = jnp.concatenate([spec[:, 1], -spec[:, 0]], axis=-1)
    count_in = left.shape[1]
    blocks = count_in // TILE
    chans = left.shape[0]
    real_rows = []
    imag_rows = []
    for first in range(blocks):
        lower = first * TILE
        cols = left[:, lower:]
        real_part = jnp.einsum(
            "cik,cjk->cij", left[:, lower : lower + TILE], cols, preferred_element_type=jnp.float32
        )
        imag_part = jnp.einsum(
            "cik,cjk->cij",
            twisted[:, lower : lower + TILE],
            cols,
            preferred_element_type=jnp.float32,
        )
        count = blocks - first
        real_rows.append(real_part.reshape(chans, TILE, count, TILE).transpose(0, 2, 1, 3))
        imag_rows.append(imag_part.reshape(chans, TILE, count, TILE).transpose(0, 2, 1, 3))
    real_all = jnp.concatenate(real_rows, axis=1)
    imag_all = jnp.concatenate(imag_rows, axis=1)
    return jnp.stack([real_all, imag_all], axis=2) * scale


def on_device(voltages, pfb_taps):
    inp_local = voltages.shape[0]
    frames_local = voltages.shape[1] // FRAME
    previous = from_behind(voltages[:, voltages.shape[1] - (TAPS - 1) * FRAME :], "tm", 1)
    extended = jnp.concatenate([previous, voltages], axis=1).reshape(
        inp_local, frames_local + TAPS - 1, FRAME
    )
    filtered = jnp.zeros((inp_local, frames_local, FRAME), jnp.float32)
    for tap in range(TAPS):
        filtered = filtered + pfb_taps[tap][None, None, :] * extended[
            :, tap : tap + frames_local, :
        ].astype(jnp.float32)
    filtered = filtered.astype(jnp.bfloat16)
    table = dft_table(F, FRAME)
    spectra = jnp.einsum("kn,itn->kit", table, filtered, preferred_element_type=jnp.float32)
    spectra = spectra.astype(jnp.bfloat16).reshape(F, 2, inp_local, frames_local)
    blocks_time = lax.axis_size("tm")
    scale = 1.0 / (frames_local * blocks_time)
    turned = lax.all_to_all(
        lax.all_to_all(spectra, "inputs", split_axis=0, concat_axis=2, tiled=True),
        "tm",
        split_axis=0,
        concat_axis=3,
        tiled=True,
    )
    return tile_sums(turned, scale)


def solution(mesh):
    in_specs = (P("inputs", "tm"), P())
    out_specs = P(("inputs", "tm"), None, None, None, None)
    return jax.shard_map(
        on_device, mesh=mesh, in_specs=in_specs, out_specs=out_specs, check_vma=False
    )
```

profile of v0, /device:TPU:0, one launch (start us, length us, event | category | flops | bytes accessed | tf_op | source)
XLA Modules:
  0.0 76.3 jit_solution(17021184768935166234)
XLA Ops:
  0.0 0.9 %slice.60 = bf16[16,3584]{1,0:T(8,128)(2,1)S(1)} slice(bf16[16,32768]{1,0:T(8,128)(2,1)} %param.2), slice={[0:16], [29184:32768]} | slice | bytes 229376 | tf_op jit(solution)/shard_map/slice | solution.py:60
  0.9 2.4 %collective-permute-start = (bf16[16,3584]{1,0:T(8,128)(2,1)S(1)}, bf16[16,3584]{1,0:T(8,128)(2,1)S(1)}, u32[]{:S(2)}, u32[]{:S(2)}) collective-permute-start(bf16[16,3584]{1,0:T(8,128)(2,1)S(1)} %slice.60), channel_id=1, source_target_pairs={{0,1},{1,2},{2,3},{4,5},{5,6},{6,7},{8,9},{9,10},{10,11},{12,13},{... | collective-permute-start | bytes 344072 | tf_op jit(solution)/shard_map/ppermute | solution.py:15
  3.3 1.0 %fusion.32 = (f32[1,512]{1,0:T(1,128)S(1)}, f32[1,512]{1,0:T(1,128)S(1)}, f32[1,512]{1,0:T(1,128)S(1)}, f32[1,512]{1,0:T(1,128)S(1)}, f32[1,512]{1,0:T(1,128)S(1...) fusion(f32[8,512]{1,0:T(8,128)} %param.3), kind=kLoop, calls=%fused_computation.48 | loop fusion | bytes 32768 | tf_op jit(solution)/shard_map/slice | solution.py:66
  4.4 0.0 collective-permute-done
  4.4 1.3 %pad_maximum_fusion = bf16[16,36352]{1,0:T(8,128)(2,1)S(1)} fusion(bf16[16,32768]{1,0:T(8,128)(2,1)} %param.2, bf16[16,3584]{1,0:T(8,128)(2,1)S(1)} %collective-permute-done), kind=kLoop, calls=%fused_computation.7 | loop fusion | flops 2326528 | bytes 2326528 | tf_op jit(solution)/shard_map/concatenate | solution.py:61
  5.7 0.7 reshape.74
  6.4 6.5 %convolution_convert_fusion = bf16[512,16,64]{0,2,1:T(8,128)(2,1)S(1)} fusion(bf16[16,71,512]{2,1,0:T(8,128)(2,1)S(1)} %reshape.74, f32[512]{0:T(512)S(1)} %bitcast.42, f32[512]{0:T(512)S(1)} %bitcast.43, f32[512]{0:T(512)S(1)} %bitcast.37, f32[512]{0:T(512)S(1)} %bitcast.38, f32[512]{0:T(512)S(1)} %bitcast.39, f32[512]{0:T(512)S(1)} %bitcast.40, ...), kind=kOutput, calls=%fused_computation.4 | convolution fusion | flops 554696704 | bytes 9456128 | tf_op jit(solution)/shard_map/kn,itn->kit/dot_general | solution.py:71
  12.9 2.0 %copy.11 = bf16[512,16,64]{2,1,0:T(8,128)(2,1)S(1)} copy(bf16[512,16,64]{0,2,1:T(8,128)(2,1)S(1)} %convolution_convert_fusion) | data formatting | bytes 2097152 | tf_op jit(solution)/shard_map/convert_element_type | solution.py:72
  15.0 1.7 %reshape.77 = bf16[8,2,32768]{2,1,0:T(2,128)(2,1)S(1)} reshape(bf16[256,2,16,64]{3,2,1,0:T(8,128)(2,1)S(1)} %bitcast.27) | data formatting | bytes 2097152
  16.7 32.5 %all_to_all.36 = bf16[8,2,32768]{2,1,0:T(2,128)(2,1)} all-to-all(bf16[8,2,32768]{2,1,0:T(2,128)(2,1)S(1)} %reshape.77), channel_id=1, replica_groups=mesh['inputs'=8,'tm'=4] {'inputs'}, dimensions={0} | all-to-all | bytes 2097152 | tf_op jit(solution)/shard_map/all_to_all | solution.py:76
  49.1 3.1 %reshape.78 = bf16[256,2,16,64]{3,2,1,0:T(8,128)(2,1)S(1)} reshape(bf16[8,2,32768]{2,1,0:T(2,128)(2,1)} %all_to_all.36) | data formatting | bytes 2097152
  52.2 2.0 %copy.12 = bf16[8,32,2,16,64]{4,3,0,2,1:T(8,128)(2,1)} copy(bf16[8,32,2,16,64]{4,3,2,1,0:T(8,128)(2,1)S(1)} %bitcast.28) | data formatting | bytes 2097152 | tf_op jit(solution)/shard_map/all_to_all | solution.py:76
  54.2 2.0 %copy.13 = bf16[32,2,128,64]{2,3,1,0:T(8,128)(2,1)S(1)} copy(bf16[32,2,128,64]{3,2,1,0:T(8,128)(2,1)} %bitcast.29) | data formatting | bytes 2097152 | tf_op jit(solution)/shard_map/all_to_all | solution.py:76
  56.2 17.4 %all_to_all.37 = bf16[32,2,128,64]{2,3,1,0:T(8,128)(2,1)S(1)} all-to-all(bf16[32,2,128,64]{2,3,1,0:T(8,128)(2,1)S(1)} %copy.13), channel_id=1, replica_groups=mesh['inputs'=8,'tm'=4] {'tm'}, dimensions={0} | all-to-all | bytes 2097152 | tf_op jit(solution)/shard_map/all_to_all | solution.py:75
  73.6 0.1 copy.14
  73.7 0.1 fusion.31
  73.8 0.2 copy.19
  74.0 0.2 copy.18
  74.3 0.4 convolution_bitcast_fusion.1
  74.7 0.4 convolution_bitcast_fusion
  75.2 0.1 maximum_multiply_fusion
  75.3 1.1 %copy.17 = f32[8,1,2,128,128]{4,3,2,1,0:T(8,128)} copy(f32[8,1,2,128,128]{4,3,0,2,1:T(8,128)S(1)} %maximum_multiply_fusion) | data formatting | bytes 2097152 | tf_op jit(solution)/shard_map/mul | solution.py:54
  (3 shorter events, 0.0 us)
Async XLA Ops:
  0.9 3.5 %collective-permute-start = (bf16[16,3584]{1,0:T(8,128)(2,1)S(1)}, bf16[16,3584]{1,0:T(8,128)(2,1)S(1)}, u32[]{:S(2)}, u32[]{:S(2)}) collective-permute-start(bf16[16,3584]{1,0:T(8,128)(2,1)S(1)} %slice.60), channel_id=1, source_target_pairs={{0,1},{1,2},{2,3},{4,5},{5,6},{6,7},{8,9},{9,10},{10,11},{12,13},{... | collective-permute-start | bytes 344072 | tf_op jit(solution)/shard_map/ppermute | solution.py:15
where the time goes:
time: 76.7 us; the launch traced here: 76.3 us
  blocking collectives  49.9 us (65%)
  local copies, waits for them, and re-layouts  15.1 us (20%)
  matrix products  7.4 us (10%)
  starting transfers between devices  2.39 us (3%)
  other arithmetic  1.43 us (2%)
    all_to_all x1, blocking collectives, on_device(): lax.all_to_all(spectra, 'inputs', split_axis=0, concat_axis=2, tiled=True)  32.5 us
    all_to_all x1, blocking collectives, on_device(): lax.all_to_all(lax.all_to_all(spectra, 'inputs', split_axis=0, concat_axi...  17.4 us
    dot_general x1, matrix products, on_device(): jnp.einsum('kn,itn->kit', table, filtered, preferred_element_type=jnp.flo...  6.55 us
    unnamed x4, local copies, waits for them, and re-layouts  5.2 us
    all_to_all x2, local copies, waits for them, and re-layouts, on_device(): lax.all_to_all(spectra, 'inputs', split_axis=0, concat_axis=2, tiled=True)  3.96 us
    ppermute x1, starting transfers between devices, from_behind(): lax.ppermute(value, axis, [(source, source + steps) for source in range(i...  2.39 us
    convert_element_type x1, local copies, waits for them, and re-layouts, on_device(): spectra.astype(jnp.bfloat16).reshape(F, 2, inp_local, frames_local)  2.03 us
  transfers between devices with their start and end apart: 1, of which 0 were waited for; matrix products, arithmetic and copies ran while one was open for 1% of the time, Pallas kernels for 0%

commit v1 on v0

--- a/solution.py
+++ b/solution.py
@@ -7,6 +7,20 @@
 TAPS = 8
 TILE = 128
 FRAME = 512
+
+
+def supply_outputs(in_array, array_dim, x0):
+    part_now = in_array.shape
+    tile_out = in_array.reshape(
+        *part_now[:array_dim], x0, part_now[array_dim] // x0, *part_now[array_dim + 1 :]
+    )
+    return jnp.moveaxis(tile_out, array_dim, 0)
+
+
+def entries_bind(packet, d0):
+    packet = jnp.moveaxis(packet, 0, d0)
+    main = packet.shape
+    return packet.reshape(*main[:d0], main[d0] * main[d0 + 1], *main[d0 + 2 :])
 
 
 def from_behind(value, axis, steps):
@@ -72,12 +86,27 @@
     spectra = spectra.astype(jnp.bfloat16).reshape(F, 2, inp_local, frames_local)
     blocks_time = lax.axis_size("tm")
     scale = 1.0 / (frames_local * blocks_time)
+
+    def launch_words_all(patch, shard_axis, local, x_part):
+        piece_now, raw_out = (lax.axis_size(shard_axis), lax.axis_index(shard_axis))
+        then = supply_outputs(patch, local, piece_now)
+        at = 1
+        buffer = [then[raw_out]]
+        while at < piece_now:
+            newest = then[(raw_out + at) % piece_now]
+            buffer.append(
+                lax.ppermute(
+                    newest,
+                    shard_axis,
+                    [(dev_i, (dev_i + at) % piece_now) for dev_i in range(piece_now)],
+                )
+            )
+            at += 1
+        then = jnp.stack(buffer)[(raw_out - jnp.arange(piece_now)) % piece_now]
+        return entries_bind(then, x_part)
+
     turned = lax.all_to_all(
-        lax.all_to_all(spectra, "inputs", split_axis=0, concat_axis=2, tiled=True),
-        "tm",
-        split_axis=0,
-        concat_axis=3,
-        tiled=True,
+        launch_words_all(spectra, "inputs", 0, 2), "tm", split_axis=0, concat_axis=3, tiled=True
     )
     return tile_sums(turned, scale)
 

time: 76.7 us -> 91.3 us (1.19)
  the two profiles are of different devices: /device:TPU:0 before, /device:TPU:12 now
where the time goes in v1:
time: 91.3 us; the launch traced here: 90.9 us
  waiting for transfers between devices  36.4 us (40%)
  local copies, waits for them, and re-layouts  18 us (20%)
  blocking collectives  16.9 us (19%)
  starting transfers between devices  10.5 us (12%)
  matrix products  7.41 us (8%)
  other arithmetic  1.45 us (2%)
    ppermute x7, waiting for transfers between devices, launch_words_all(): lax.ppermute(newest, shard_axis, [(dev_i, (dev_i + at) % piece_now) for d...  36.4 us
    all_to_all x1, blocking collectives, on_device(): lax.all_to_all(launch_words_all(spectra, 'inputs', 0, 2), 'tm', split_axi...  16.9 us
    ppermute x7, starting transfers between devices, launch_words_all(): lax.ppermute(newest, shard_axis, [(dev_i, (dev_i + at) % piece_now) for d...  8.74 us
    dot_general x1, matrix products, on_device(): jnp.einsum('kn,itn->kit', table, filtered, preferred_element_type=jnp.flo...  6.55 us
    unnamed x9, local copies, waits for them, and re-layouts  5.56 us
    gather x1, local copies, waits for them, and re-layouts, launch_words_all(): then = jnp.stack(buffer)[(raw_out - jnp.arange(piece_now)) % piece_now]  2.54 us
    reshape x1, local copies, waits for them, and re-layouts, entries_bind(): return packet.reshape(*main[:d0], main[d0] * main[d0 + 1], *main[d0 + 2:])  2.13 us
    convert_element_type x1, local copies, waits for them, and re-layouts, on_device(): spectra.astype(jnp.bfloat16).reshape(F, 2, inp_local, frames_local)  2.03 us
  transfers between devices with their start and end apart: 8, of which 5 were waited for; matrix products, arithmetic and copies ran while one was open for 8% of the time, Pallas kernels for 0%

profile of v1, /device:TPU:12, one launch (start us, length us, event | category | flops | bytes accessed | tf_op | source)
XLA Modules:
  0.0 90.9 jit_solution(11254391473375022890)
XLA Ops:
  0.0 0.9 slice.60
  0.9 1.7 %collective-permute-start = (bf16[16,3584]{1,0:T(8,128)(2,1)S(1)}, bf16[16,3584]{1,0:T(8,128)(2,1)S(1)}, u32[]{:S(2)}, u32[]{:S(2)}) collective-permute-start(bf16[16,3584]{1,0:T(8,128)(2,1)S(1)} %slice.60), channel_id=1, source_target_pairs={{0,1},{1,2},{2,3},{4,5},{5,6},{6,7},{8,9},{9,10},{10,11},{12,13},{... | collective-permute-start | bytes 344072 | tf_op jit(solution)/shard_map/ppermute | solution.py:29
  2.7 1.0 %fusion.34 = (f32[1,512]{1,0:T(1,128)S(1)}, f32[1,512]{1,0:T(1,128)S(1)}, f32[1,512]{1,0:T(1,128)S(1)}, f32[1,512]{1,0:T(1,128)S(1)}, f32[1,512]{1,0:T(1,128)S(1...) fusion(f32[8,512]{1,0:T(8,128)} %param.3), kind=kLoop, calls=%fused_computation.79 | loop fusion | bytes 32768 | tf_op jit(solution)/shard_map/slice | solution.py:80
  3.9 1.3 %pad_maximum_fusion = bf16[16,36352]{1,0:T(8,128)(2,1)S(1)} fusion(bf16[16,32768]{1,0:T(8,128)(2,1)} %param.2, bf16[16,3584]{1,0:T(8,128)(2,1)S(1)} %collective-permute-done), kind=kLoop, calls=%fused_computation.8 | loop fusion | flops 2326528 | bytes 2326528 | tf_op jit(solution)/shard_map/concatenate | solution.py:75
  5.9 6.5 %convolution_convert_fusion = bf16[512,16,64]{0,2,1:T(8,128)(2,1)S(1)} fusion(bf16[16,71,512]{2,1,0:T(8,128)(2,1)S(1)} %reshape.123, f32[512]{0:T(512)S(1)} %bitcast.84, f32[512]{0:T(512)S(1)} %bitcast.85, f32[512]{0:T(512)S(1)} %bitcast.79, f32[512]{0:T(512)S(1)} %bitcast.80, f32[512]{0:T(512)S(1)} %bitcast.81, f32[512]{0:T(512)S(1)} %bitcast.82, ...), kind=kOutput, calls=%fused_computation.5 | convolution fusion | flops 554696704 | bytes 9456128 | tf_op jit(solution)/shard_map/kn,itn->kit/dot_general | solution.py:85
  12.4 2.0 %copy.4 = bf16[512,16,64]{2,1,0:T(8,128)(2,1)S(1)} copy(bf16[512,16,64]{0,2,1:T(8,128)(2,1)S(1)} %convolution_convert_fusion) | data formatting | bytes 2097152 | tf_op jit(solution)/shard_map/convert_element_type | solution.py:86
  15.0 1.6 %collective-permute-start.1 = (bf16[32,2,16,64]{3,0,1,2:T(8,128)(2,1)S(1)}, bf16[32,2,16,64]{3,0,1,2:T(8,128)(2,1)S(1)}, u32[]{:S(2)}, u32[]{:S(2)}) collective-permute-start(bf16[32,2,16,64]{3,0,1,2:T(8,128)(2,1)S(1)} %bitcast.77), channel_id=1, source_target_pairs={{0,4},{4,8},{8,12},{12,16},{16,20},{20,24},{24,28},{28,0},{1,5},{5... | collective-permute-start | bytes 393224 | tf_op jit(solution)/shard_map/ppermute | solution.py:98
  16.7 1.6 %collective-permute-start.2 = (bf16[32,2,16,64]{3,0,1,2:T(8,128)(2,1)S(1)}, bf16[32,2,16,64]{3,0,1,2:T(8,128)(2,1)S(1)}, u32[]{:S(2)}, u32[]{:S(2)}) collective-permute-start(bf16[32,2,16,64]{3,0,1,2:T(8,128)(2,1)S(1)} %bitcast.76), channel_id=1, source_target_pairs={{0,8},{4,12},{8,16},{12,20},{16,24},{20,28},{24,0},{28,4},{1,9},{5... | collective-permute-start | bytes 393224 | tf_op jit(solution)/shard_map/ppermute | solution.py:98
  18.4 1.2 %collective-permute-start.3 = (bf16[32,2,16,64]{3,0,1,2:T(8,128)(2,1)S(1)}, bf16[32,2,16,64]{3,0,1,2:T(8,128)(2,1)S(1)}, u32[]{:S(2)}, u32[]{:S(2)}) collective-permute-start(bf16[32,2,16,64]{3,0,1,2:T(8,128)(2,1)S(1)} %bitcast.75), channel_id=1, source_target_pairs={{0,12},{4,16},{8,20},{12,24},{16,28},{20,0},{24,4},{28,8},{1,13},{... | collective-permute-start | bytes 393224 | tf_op jit(solution)/shard_map/ppermute | solution.py:98
  19.7 1.8 %collective-permute-start.4 = (bf16[32,2,16,64]{3,0,1,2:T(8,128)(2,1)S(1)}, bf16[32,2,16,64]{3,0,1,2:T(8,128)(2,1)S(1)}, u32[]{:S(2)}, u32[]{:S(2)}) collective-permute-start(bf16[32,2,16,64]{3,0,1,2:T(8,128)(2,1)S(1)} %bitcast.74), channel_id=1, source_target_pairs={{0,16},{4,20},{8,24},{12,28},{16,0},{20,4},{24,8},{28,12},{1,17},{... | collective-permute-start | bytes 393224 | tf_op jit(solution)/shard_map/ppermute | solution.py:98
  21.6 1.3 %collective-permute-start.5 = (bf16[32,2,16,64]{3,0,1,2:T(8,128)(2,1)S(1)}, bf16[32,2,16,64]{3,0,1,2:T(8,128)(2,1)S(1)}, u32[]{:S(2)}, u32[]{:S(2)}) collective-permute-start(bf16[32,2,16,64]{3,0,1,2:T(8,128)(2,1)S(1)} %bitcast.73), channel_id=1, source_target_pairs={{0,20},{4,24},{8,28},{12,0},{16,4},{20,8},{24,12},{28,16},{1,21},{... | collective-permute-start | bytes 393224 | tf_op jit(solution)/shard_map/ppermute | solution.py:98
  23.2 0.8 copy_dynamic-update-slice_fusion
  24.0 1.2 %collective-permute-start.6 = (bf16[32,2,16,64]{3,0,1,2:T(8,128)(2,1)S(1)}, bf16[32,2,16,64]{3,0,1,2:T(8,128)(2,1)S(1)}, u32[]{:S(2)}, u32[]{:S(2)}) collective-permute-start(bf16[32,2,16,64]{3,0,1,2:T(8,128)(2,1)S(1)} %bitcast.72), channel_id=1, source_target_pairs={{0,24},{4,28},{8,0},{12,4},{16,8},{20,12},{24,16},{28,20},{1,25},{... | collective-permute-start | bytes 393224 | tf_op jit(solution)/shard_map/ppermute | solution.py:98
  25.9 2.5 %collective-permute-done.2 = bf16[32,2,16,64]{3,0,1,2:T(8,128)(2,1)S(1)} collective-permute-done((bf16[32,2,16,64]{3,0,1,2:T(8,128)(2,1)S(1)}, bf16[32,2,16,64]{3,0,1,2:T(8,128)(2,1)S(1)}, u32[]{:S(2)}, u32[]{:S(2)}) %collective-permute-start.2) | collective-permute-done | bytes 131104 | tf_op jit(solution)/shard_map/ppermute | solution.py:98
  29.1 26.5 %collective-permute-done.3 = bf16[32,2,16,64]{3,0,1,2:T(8,128)(2,1)S(1)} collective-permute-done((bf16[32,2,16,64]{3,0,1,2:T(8,128)(2,1)S(1)}, bf16[32,2,16,64]{3,0,1,2:T(8,128)(2,1)S(1)}, u32[]{:S(2)}, u32[]{:S(2)}) %collective-permute-start.3) | collective-permute-done | bytes 131104 | tf_op jit(solution)/shard_map/ppermute | solution.py:98
  56.3 4.9 %collective-permute-done.4 = bf16[32,2,16,64]{3,0,1,2:T(8,128)(2,1)S(1)} collective-permute-done((bf16[32,2,16,64]{3,0,1,2:T(8,128)(2,1)S(1)}, bf16[32,2,16,64]{3,0,1,2:T(8,128)(2,1)S(1)}, u32[]{:S(2)}, u32[]{:S(2)}) %collective-permute-start.4) | collective-permute-done | bytes 131104 | tf_op jit(solution)/shard_map/ppermute | solution.py:98
  61.9 0.7 bitcast_dynamic-update-slice_fusion.2
  62.7 1.4 %collective-permute-done.6 = bf16[32,2,16,64]{3,0,1,2:T(8,128)(2,1)S(1)} collective-permute-done((bf16[32,2,16,64]{3,0,1,2:T(8,128)(2,1)S(1)}, bf16[32,2,16,64]{3,0,1,2:T(8,128)(2,1)S(1)}, u32[]{:S(2)}, u32[]{:S(2)}) %collective-permute-start.6) | collective-permute-done | bytes 131104 | tf_op jit(solution)/shard_map/ppermute | solution.py:98
  64.8 1.1 %collective-permute-done.7 = bf16[32,2,16,64]{3,0,1,2:T(8,128)(2,1)S(1)} collective-permute-done((bf16[32,2,16,64]{3,0,1,2:T(8,128)(2,1)S(1)}, bf16[32,2,16,64]{3,0,1,2:T(8,128)(2,1)S(1)}, u32[]{:S(2)}, u32[]{:S(2)}) %collective-permute-start.7) | collective-permute-done | bytes 131104 | tf_op jit(solution)/shard_map/ppermute | solution.py:98
  65.9 0.7 bitcast_dynamic-update-slice_fusion
  66.7 2.5 %gather_fusion = bf16[8,32,2,16,64]{4,1,2,3,0:T(8,128)(2,1)S(1)} fusion(bf16[8,32,2,16,64]{4,1,2,3,0:T(8,128)(2,1)} %bitcast_dynamic-update-slice_fusion, s32[1024]{0:T(1024)S(1)} %pad_clamp_fusion), kind=kCustom, calls=%fused_computation | custom fusion | bytes 2097184 | tf_op jit(solution)/shard_map/gather | solution.py:105
  69.2 2.1 %copy.13 = bf16[32,2,128,64]{2,3,1,0:T(8,128)(2,1)S(1)} copy(bf16[32,2,128,64]{3,0,1,2:T(8,128)(2,1)S(1)} %bitcast.64) | data formatting | bytes 2097152 | tf_op jit(solution)/shard_map/reshape | solution.py:23
  71.4 16.9 %all_to_all.18 = bf16[32,2,128,64]{2,3,1,0:T(8,128)(2,1)S(1)} all-to-all(bf16[32,2,128,64]{2,3,1,0:T(8,128)(2,1)S(1)} %copy.13), channel_id=1, replica_groups=mesh['inputs'=8,'tm'=4] {'tm'}, dimensions={0} | all-to-all | bytes 2097152 | tf_op jit(solution)/shard_map/all_to_all | solution.py:108
  89.9 1.1 %copy.17 = f32[8,1,2,128,128]{4,3,2,1,0:T(8,128)} copy(f32[8,1,2,128,128]{4,3,0,2,1:T(8,128)S(1)} %maximum_multiply_fusion) | data formatting | bytes 2097152 | tf_op jit(solution)/shard_map/mul | solution.py:68
  (30 shorter events, 7.0 us)
Async XLA Ops:
  0.9 3.0 %collective-permute-start = (bf16[16,3584]{1,0:T(8,128)(2,1)S(1)}, bf16[16,3584]{1,0:T(8,128)(2,1)S(1)}, u32[]{:S(2)}, u32[]{:S(2)}) collective-permute-start(bf16[16,3584]{1,0:T(8,128)(2,1)S(1)} %slice.60), channel_id=1, source_target_pairs={{0,1},{1,2},{2,3},{4,5},{5,6},{6,7},{8,9},{9,10},{10,11},{12,13},{... | collective-permute-start | bytes 344072 | tf_op jit(solution)/shard_map/ppermute | solution.py:29
  15.0 9.0 %collective-permute-start.1 = (bf16[32,2,16,64]{3,0,1,2:T(8,128)(2,1)S(1)}, bf16[32,2,16,64]{3,0,1,2:T(8,128)(2,1)S(1)}, u32[]{:S(2)}, u32[]{:S(2)}) collective-permute-start(bf16[32,2,16,64]{3,0,1,2:T(8,128)(2,1)S(1)} %bitcast.77), channel_id=1, source_target_pairs={{0,4},{4,8},{8,12},{12,16},{16,20},{20,24},{24,28},{28,0},{1,5},{5... | collective-permute-start | bytes 393224 | tf_op jit(solution)/shard_map/ppermute | solution.py:98
  16.7 11.8 %collective-permute-start.2 = (bf16[32,2,16,64]{3,0,1,2:T(8,128)(2,1)S(1)}, bf16[32,2,16,64]{3,0,1,2:T(8,128)(2,1)S(1)}, u32[]{:S(2)}, u32[]{:S(2)}) collective-permute-start(bf16[32,2,16,64]{3,0,1,2:T(8,128)(2,1)S(1)} %bitcast.76), channel_id=1, source_target_pairs={{0,8},{4,12},{8,16},{12,20},{16,24},{20,28},{24,0},{28,4},{1,9},{5... | collective-permute-start | bytes 393224 | tf_op jit(solution)/shard_map/ppermute | solution.py:98
  18.4 37.2 %collective-permute-start.3 = (bf16[32,2,16,64]{3,0,1,2:T(8,128)(2,1)S(1)}, bf16[32,2,16,64]{3,0,1,2:T(8,128)(2,1)S(1)}, u32[]{:S(2)}, u32[]{:S(2)}) collective-permute-start(bf16[32,2,16,64]{3,0,1,2:T(8,128)(2,1)S(1)} %bitcast.75), channel_id=1, source_target_pairs={{0,12},{4,16},{8,20},{12,24},{16,28},{20,0},{24,4},{28,8},{1,13},{... | collective-permute-start | bytes 393224 | tf_op jit(solution)/shard_map/ppermute | solution.py:98
  19.7 41.5 %collective-permute-start.4 = (bf16[32,2,16,64]{3,0,1,2:T(8,128)(2,1)S(1)}, bf16[32,2,16,64]{3,0,1,2:T(8,128)(2,1)S(1)}, u32[]{:S(2)}, u32[]{:S(2)}) collective-permute-start(bf16[32,2,16,64]{3,0,1,2:T(8,128)(2,1)S(1)} %bitcast.74), channel_id=1, source_target_pairs={{0,16},{4,20},{8,24},{12,28},{16,0},{20,4},{24,8},{28,12},{1,17},{... | collective-permute-start | bytes 393224 | tf_op jit(solution)/shard_map/ppermute | solution.py:98
  21.6 40.4 %collective-permute-start.5 = (bf16[32,2,16,64]{3,0,1,2:T(8,128)(2,1)S(1)}, bf16[32,2,16,64]{3,0,1,2:T(8,128)(2,1)S(1)}, u32[]{:S(2)}, u32[]{:S(2)}) collective-permute-start(bf16[32,2,16,64]{3,0,1,2:T(8,128)(2,1)S(1)} %bitcast.73), channel_id=1, source_target_pairs={{0,20},{4,24},{8,28},{12,0},{16,4},{20,8},{24,12},{28,16},{1,21},{... | collective-permute-start | bytes 393224 | tf_op jit(solution)/shard_map/ppermute | solution.py:98
  24.0 40.1 %collective-permute-start.6 = (bf16[32,2,16,64]{3,0,1,2:T(8,128)(2,1)S(1)}, bf16[32,2,16,64]{3,0,1,2:T(8,128)(2,1)S(1)}, u32[]{:S(2)}, u32[]{:S(2)}) collective-permute-start(bf16[32,2,16,64]{3,0,1,2:T(8,128)(2,1)S(1)} %bitcast.72), channel_id=1, source_target_pairs={{0,24},{4,28},{8,0},{12,4},{16,8},{20,12},{24,16},{28,20},{1,25},{... | collective-permute-start | bytes 393224 | tf_op jit(solution)/shard_map/ppermute | solution.py:98
  28.4 37.5 %collective-permute-start.7 = (bf16[32,2,16,64]{3,0,1,2:T(8,128)(2,1)S(1)}, bf16[32,2,16,64]{3,0,1,2:T(8,128)(2,1)S(1)}, u32[]{:S(2)}, u32[]{:S(2)}) collective-permute-start(bf16[32,2,16,64]{3,0,1,2:T(8,128)(2,1)S(1)} %bitcast.71), channel_id=1, source_target_pairs={{0,28},{4,0},{8,4},{12,8},{16,12},{20,16},{24,20},{28,24},{1,29},{... | collective-permute-start | bytes 393224 | tf_op jit(solution)/shard_map/ppermute | solution.py:98
